TPU v7x, 32 devices: a whole 2x2x4 slice. The times are simulated.
32 devices in a mesh: groups: 2 (over y), ctx: 4 (over x, core), dp: 4 (over z).
Axes of the slice: x: 2, y: 2, z: 4, core: 2. Of those that a mesh axis runs over, the one named last changes fastest.
Arguments:
- tokens: bfloat16 [8, 512, 1024], P(('groups', 'dp'), 'ctx'), parts along dimension 0, may hold values from -24 to 24
- global_blocks: int32 [8, 2], P(('groups', 'dp')), parts along dimension 0, may hold values from 0 to 7, as said below
- w_query: bfloat16 [1024, 1024], P('dp'), may hold values from -0.125 to 0.125
- w_key: bfloat16 [1024, 1024], P('dp'), may hold values from -0.125 to 0.125
- w_value: bfloat16 [1024, 1024], P('dp'), may hold values from -0.1875 to 0.1875
- d_context: bfloat16 [8, 512, 1024], P(('groups', 'dp'), 'ctx'), parts along dimension 0, may hold values from -6 to 6
Outputs:
- context: bfloat16 [8, 512, 1024], P(('groups', 'dp'), 'ctx'), parts along dimension 0
- grad_tokens: bfloat16 [8, 512, 1024], P(('groups', 'dp'), 'ctx'), parts along dimension 0
- grad_w_query: float32 [2048, 1024], P(('groups', 'dp'), 'ctx'), parts along dimension 0
- grad_w_key: float32 [2048, 1024], P(('groups', 'dp'), 'ctx'), parts along dimension 0
- grad_w_value: float32 [2048, 1024], P(('groups', 'dp'), 'ctx'), parts along dimension 0
There are 2 independent parts, one for each index of `groups`. A program takes and returns all parts, laid end to end along the dimension named above; an argument that names none is the same for every part. Nothing has to cross between parts.
Inputs may be any that keep to these rules, and one draw needn't show every extreme that they name: `global_blocks`: each sequence names two different blocks.
All inputs are finite; a program needn't handle non-finite values.
Results may differ from a plain program's by a relative error of at most 0.015.
The roundings to bfloat16 on the way count: a program that leaves them out, or rounds other values in their place, can miss the bound.
Values may be sent and summed in bfloat16 or wider, within the bound.
No kernel may reach another device: no remote copies, remote signals or barrier semaphores. Data moves between devices by JAX's collectives and lax.ppermute only.
A program may use at most 128 MiB of HBM per device.

v0:
```python
import math
import jax
import jax.numpy as jnp
from jax import lax
from jax.sharding import PartitionSpec as P

HEADS = 16
BLK = 64
NEG = -1e30


def with_halo(block, sides, width):
    for axis, dim in sides:
        count = lax.axis_size(axis)
        forward = [(i, i + 1) for i in range(count - 1)]
        backward = [(target, source) for source, target in forward]
        low = lax.ppermute(
            lax.slice_in_dim(block, block.shape[dim] - width, None, axis=dim), axis, forward
        )
        high = lax.ppermute(lax.slice_in_dim(block, 0, width, axis=dim), axis, backward)
        block = jnp.concatenate([low, block, high], axis=dim)
    return block


def block_masks(first_block, block_count, all_blocks, chosen_blocks):
    blocks = first_block + jnp.arange(block_count, dtype=jnp.int32)
    near = blocks[:, None] - 1 + jnp.arange(3, dtype=jnp.int32)[None, :]
    near_ok = (near >= 0) & (near < all_blocks)
    far_ok = jnp.abs(chosen_blocks[None, :] - blocks[:, None]) > 1
    near_keep = jnp.repeat(near_ok, BLK, axis=1)
    far_keep = jnp.repeat(far_ok, BLK, axis=1)
    chosen = (blocks == chosen_blocks[0]) | (blocks == chosen_blocks[1])
    return (near_keep, far_keep, chosen)


def per_device(tokens, global_blocks, w_query, w_key, w_value, d_context):
    inputs = tokens[0]
    upstream = d_context[0]
    tokens_here, model_width = inputs.shape
    hdim = model_width // HEADS
    block_count = tokens_here // BLK
    score_scale = 1.0 / math.sqrt(hdim)
    position = lax.axis_index("ctx")
    all_blocks = lax.axis_size("ctx") * block_count
    chosen_blocks = global_blocks[0]
    pieces = (
        lax.all_gather(w_query, "dp", axis=0, tiled=True),
        lax.all_gather(w_key, "dp", axis=0, tiled=True),
        lax.all_gather(w_value, "dp", axis=0, tiled=True),
    )
    projected = tuple(
        (jnp.dot(inputs, piece, preferred_element_type=jnp.float32) for piece in pieces)
    )
    queries, key_rows, value_rows = [values.astype(jnp.bfloat16) for values in projected]
    owner = chosen_blocks // block_count
    local_index = chosen_blocks - owner * block_count
    mine = owner == position
    block_ids = jnp.arange(block_count, dtype=jnp.int32)

    def pick_rows(matrix):
        blocked = matrix.reshape(block_count, BLK, model_width)
        pieces = []
        for which in range(2):
            piece = lax.dynamic_slice_in_dim(blocked, local_index[which], 1, 0)[0]
            pieces.append(jnp.where(mine[which], piece, jnp.zeros_like(piece)).astype(jnp.float32))
        return jnp.concatenate(pieces, axis=0)

    picked = jnp.stack([pick_rows(queries), pick_rows(key_rows), pick_rows(value_rows)])
    shared_rows, shared_up = (
        lax.psum(picked.astype(jnp.bfloat16), "ctx").astype(jnp.float32),
        lax.psum(pick_rows(upstream).astype(jnp.bfloat16), "ctx").astype(jnp.float32),
    )
    shared_rows = shared_rows.astype(jnp.bfloat16)
    global_query = shared_rows[0].reshape(2 * BLK, HEADS, hdim)
    far_key = shared_rows[1].reshape(2 * BLK, HEADS, hdim)
    far_value = shared_rows[2].reshape(2 * BLK, HEADS, hdim)
    global_up = shared_up.astype(jnp.bfloat16).reshape(2 * BLK, HEADS, hdim)
    padded = with_halo(jnp.stack([key_rows, value_rows]), (("ctx", 1),), BLK)
    padded = padded.reshape(2, block_count + 2, BLK, model_width)

    def near_rows(side):
        return jnp.concatenate([side[:-2], side[1:-1], side[2:]], axis=1).reshape(
            block_count, 3 * BLK, HEADS, hdim
        )

    near_key = near_rows(padded[0])
    near_value = near_rows(padded[1])
    near_keep, far_keep, chosen = block_masks(
        position * block_count, block_count, all_blocks, chosen_blocks
    )
    query_heads = queries.reshape(block_count, BLK, HEADS, hdim)
    near_scores = (
        jnp.einsum("nqhe,nkhe->nhqk", query_heads, near_key, preferred_element_type=jnp.float32)
        * score_scale
    )
    near_scores = jnp.where(near_keep[:, None, None, :], near_scores, NEG)
    far_scores = (
        jnp.einsum("nqhe,khe->nhqk", query_heads, far_key, preferred_element_type=jnp.float32)
        * score_scale
    )
    far_scores = jnp.where(far_keep[:, None, None, :], far_scores, NEG)
    row_max = jnp.maximum(
        jnp.max(near_scores, axis=-1, keepdims=True), jnp.max(far_scores, axis=-1, keepdims=True)
    )
    near_raw = jnp.exp(near_scores - row_max)
    far_raw = jnp.exp(far_scores - row_max)
    row_sum = jnp.sum(near_raw, axis=-1, keepdims=True) + jnp.sum(far_raw, axis=-1, keepdims=True)
    window_out = jnp.einsum(
        "nhqk,nkhe->nqhe",
        near_raw.astype(jnp.bfloat16),
        near_value,
        preferred_element_type=jnp.float32,
    )
    window_out = window_out + jnp.einsum(
        "nhqk,khe->nqhe",
        far_raw.astype(jnp.bfloat16),
        far_value,
        preferred_element_type=jnp.float32,
    )
    window_out = window_out / jnp.transpose(row_sum, (0, 2, 1, 3))
    key_heads = key_rows.reshape(tokens_here, HEADS, hdim)
    value_heads = value_rows.reshape(tokens_here, HEADS, hdim)
    global_scores = (
        jnp.einsum("qhe,khe->hqk", global_query, key_heads, preferred_element_type=jnp.float32)
        * score_scale
    )
    global_max = lax.pmax(jnp.max(global_scores, axis=-1), "ctx")
    global_raw = jnp.exp(global_scores - global_max[..., None])
    part_sum = jnp.sum(global_raw, axis=-1)
    part_out = jnp.einsum(
        "hqk,khe->qhe",
        global_raw.astype(jnp.bfloat16),
        value_heads,
        preferred_element_type=jnp.float32,
    )
    global_sum, global_acc = lax.psum((part_sum, part_out), "ctx")
    global_out = global_acc / jnp.transpose(global_sum)[:, :, None]
    merged = window_out.reshape(block_count, BLK, model_width)
    global_blocks_out = global_out.reshape(2, BLK, model_width)
    for which in range(2):
        hit = (block_ids == local_index[which]) & mine[which]
        merged = jnp.where(hit[:, None, None], global_blocks_out[which][None], merged)
    context = merged.reshape(tokens_here, model_width).astype(jnp.bfloat16)
    up_heads = upstream.reshape(block_count, BLK, HEADS, hdim)
    window_up = jnp.where(chosen[:, None, None, None], jnp.zeros_like(up_heads), up_heads)
    near_probs = near_raw / row_sum
    far_probs = far_raw / row_sum
    delta = jnp.transpose(jnp.sum(window_up.astype(jnp.float32) * window_out, axis=-1), (0, 2, 1))[
        ..., None
    ]
    near_grad_probs = jnp.einsum(
        "nqhe,nkhe->nhqk", window_up, near_value, preferred_element_type=jnp.float32
    )
    far_grad_probs = jnp.einsum(
        "nqhe,khe->nhqk", window_up, far_value, preferred_element_type=jnp.float32
    )
    near_low = (near_probs * (near_grad_probs - delta)).astype(jnp.bfloat16)
    far_low = (far_probs * (far_grad_probs - delta)).astype(jnp.bfloat16)
    grad_query = jnp.einsum(
        "nhqk,nkhe->nqhe", near_low, near_key, preferred_element_type=jnp.float32
    )
    grad_query = score_scale * (
        grad_query
        + jnp.einsum("nhqk,khe->nqhe", far_low, far_key, preferred_element_type=jnp.float32)
    )
    near_grad_keys = score_scale * jnp.einsum(
        "nhqk,nqhe->nkhe", near_low, query_heads, preferred_element_type=jnp.float32
    )
    near_grad_values = jnp.einsum(
        "nhqk,nqhe->nkhe",
        near_probs.astype(jnp.bfloat16),
        window_up,
        preferred_element_type=jnp.float32,
    )
    stacked = jnp.stack([near_grad_keys, near_grad_values]).reshape(
        2, block_count, 3, BLK, model_width
    )
    left_part = stacked[:, :, 0]
    centre_part = stacked[:, :, 1]
    right_part = stacked[:, :, 2]
    zero_block = jnp.zeros((2, 1, BLK, model_width), jnp.float32)
    inner = (
        centre_part
        + jnp.concatenate([left_part[:, 1:], zero_block], axis=1)
        + jnp.concatenate([zero_block, right_part[:, :-1]], axis=1)
    )
    edges = jnp.concatenate([left_part[:, 0], right_part[:, -1]], axis=1)
    returned = with_halo(edges.astype(jnp.bfloat16), (("ctx", 1),), BLK).astype(edges.dtype)
    inner = inner.at[:, 0].add(returned[:, :BLK]).at[:, -1].add(returned[:, 3 * BLK :])
    far_grad_keys = score_scale * jnp.einsum(
        "nhqk,nqhe->khe", far_low, query_heads, preferred_element_type=jnp.float32
    )
    far_grad_values = jnp.einsum(
        "nhqk,nqhe->khe",
        far_probs.astype(jnp.bfloat16),
        window_up,
        preferred_element_type=jnp.float32,
    )
    global_probs = global_raw / global_sum[..., None]
    global_grad_probs = jnp.einsum(
        "qhe,khe->hqk", global_up, value_heads, preferred_element_type=jnp.float32
    )
    global_delta = jnp.transpose(jnp.sum(global_up.astype(jnp.float32) * global_out, axis=-1))
    global_low = (global_probs * (global_grad_probs - global_delta[..., None])).astype(jnp.bfloat16)
    part_query_grad = score_scale * jnp.einsum(
        "hqk,khe->qhe", global_low, key_heads, preferred_element_type=jnp.float32
    )
    key_from_global = score_scale * jnp.einsum(
        "hqk,qhe->khe", global_low, global_query, preferred_element_type=jnp.float32
    )
    value_from_global = jnp.einsum(
        "hqk,qhe->khe",
        global_probs.astype(jnp.bfloat16),
        global_up,
        preferred_element_type=jnp.float32,
    )
    gathered_grads = lax.psum(
        jnp.stack(
            [
                part_query_grad.reshape(2 * BLK, model_width),
                far_grad_keys.reshape(2 * BLK, model_width),
                far_grad_values.reshape(2 * BLK, model_width),
            ]
        ).astype(jnp.bfloat16),
        "ctx",
    ).astype(jnp.float32)
    grad_q = grad_query.reshape(block_count, BLK, model_width)
    grad_k = inner[0] + key_from_global.reshape(block_count, BLK, model_width)
    grad_v = inner[1] + value_from_global.reshape(block_count, BLK, model_width)
    for which in range(2):
        hit = ((block_ids == local_index[which]) & mine[which])[:, None, None]
        rows_now = gathered_grads[:, which * BLK : (which + 1) * BLK]
        grad_q = grad_q + jnp.where(hit, rows_now[0][None], 0.0)
        grad_k = grad_k + jnp.where(hit, rows_now[1][None], 0.0)
        grad_v = grad_v + jnp.where(hit, rows_now[2][None], 0.0)
    grads_low = [
        grad.reshape(tokens_here, model_width).astype(jnp.bfloat16)
        for grad in (grad_q, grad_k, grad_v)
    ]
    pieces = lax.all_gather((w_query, w_key, w_value), "dp", axis=0, tiled=True)
    result = jnp.zeros((tokens_here, pieces[0].shape[0]), jnp.float32)
    for grad, piece in zip(grads_low, pieces):
        result = result + lax.dot_general(
            grad, piece, (((1,), (1,)), ((), ())), preferred_element_type=jnp.float32
        )
    grad_tokens = result.astype(jnp.bfloat16)
    reduced = lax.psum_scatter(
        jnp.concatenate(
            [
                lax.dot_general(
                    grad, inputs, (((0,), (0,)), ((), ())), preferred_element_type=jnp.float32
                )
                for grad in grads_low
            ],
            axis=1,
        ).astype(jnp.bfloat16),
        "ctx",
        scatter_dimension=0,
        tiled=True,
    ).astype(jnp.float32)
    reduced = reduced.reshape(reduced.shape[0], 3, model_width)
    final = lax.psum_scatter(
        reduced.astype(jnp.bfloat16), "dp", scatter_dimension=2, tiled=True
    ).astype(jnp.float32)
    results = [jnp.transpose(final[:, which]) for which in range(3)]
    return (context[None], grad_tokens[None], results[0], results[1], results[2])


def solution(mesh):
    return jax.shard_map(
        per_device,
        mesh=mesh,
        in_specs=(
            P(("groups", "dp"), "ctx", None),
            P(("groups", "dp"), None),
            P("dp", None),
            P("dp", None),
            P("dp", None),
            P(("groups", "dp"), "ctx", None),
        ),
        out_specs=(
            P(("groups", "dp"), "ctx", None),
            P(("groups", "dp"), "ctx", None),
            P(("groups", "dp"), "ctx"),
            P(("groups", "dp"), "ctx"),
            P(("groups", "dp"), "ctx"),
        ),
        check_vma=False,
    )
```

profile of v0, /device:TPU:0, one launch (start us, length us, event | category | flops | bytes accessed | tf_op | source)
XLA Modules:
  0.0 460.4 jit_solution(10598500525040581107)
XLA Ops:
  19.6 2.5 compare_and_fusion.1
  22.7 35.5 %all-gather.4.cloned.1.call-done = bf16[1024,1024]{1,0:T(8,128)(2,1)} async-done(((bf16[256,1024]{1,0:T(8,128)(2,1)}), bf16[1024,1024]{1,0:T(8,128)(2,1)}) %all-gather.4.cloned.1.call-update) | async-done | bytes 2097168 | tf_op jit(solution)/shard_map/all_gather | solution.py:49
  60.3 44.5 %all-gather.8.cloned.1.call-done = bf16[1024,1024]{1,0:T(8,128)(2,1)} async-done(((bf16[256,1024]{1,0:T(8,128)(2,1)}), bf16[1024,1024]{1,0:T(8,128)(2,1)}) %all-gather.8.cloned.1.call-update) | async-done | bytes 2097168 | tf_op jit(solution)/shard_map/all_gather | solution.py:48
  107.7 2.4 collective-permute-start
  111.4 39.7 %all-gather.6.cloned.1.call-done = bf16[1024,1024]{1,0:T(8,128)(2,1)} async-done(((bf16[256,1024]{1,0:T(8,128)(2,1)}), bf16[1024,1024]{1,0:T(8,128)(2,1)}) %all-gather.6.cloned.1.call-update) | async-done | bytes 2097168 | tf_op jit(solution)/shard_map/all_gather | solution.py:47
  172.1 3.5 fusion
  175.5 17.1 %all-reduce.11.cloned.1.call-done = (bf16[3,128,1024]{2,1,0:T(8,128)(2,1)}, bf16[128,16,64]{0,2,1:T(8,128)(2,1)}) async-done(((bf16[3,128,1024]{2,1,0:T(8,128)(2,1)}, bf16[128,16,64]{0,2,1:T(8,128)(2,1)}), (bf16[3,128,1024]{2,1,0:T(8,128)(2,1)}, bf16[128,16,64]{0,2,1:T(8,128)(2,1)})) %all-reduce.11.cloned.1.call-update) | async-done | bytes 1048592 | tf_op jit(solution)/shard_map/psum | solution.py:70
  195.6 2.5 fusion.14
  209.9 2.8 copy.198
  212.7 2.9 stack.46
  215.6 3.9 copy.199
  219.5 3.7 stack.47
  229.9 6.1 %pmax.7 = f32[16,128]{1,0:T(8,128)S(1)} all-reduce(f32[16,128]{1,0:T(8,128)S(1)} %get-tuple-element.91), channel_id=1, replica_groups=mesh['groups'=2,'ctx'=4,'dp'=4] {'ctx'}, use_global_device_ids=true, to_apply=%region_2.3 | all-reduce | flops 2048 | bytes 16384 | tf_op jit(solution)/shard_map/pmax | solution.py:127
  236.2 6.0 %psum.37 = f32[16,128]{1,0:T(8,128)S(1)} all-reduce(f32[16,128]{1,0:T(8,128)S(1)} %fusion.26), channel_id=1, replica_groups=mesh['groups'=2,'ctx'=4,'dp'=4] {'ctx'}, use_global_device_ids=true, to_apply=%region_5.6 | all-reduce | flops 2048 | bytes 16384 | tf_op jit(solution)/shard_map/psum | solution.py:136
  247.5 2.2 collective-permute-start.2
  256.7 21.1 %all-reduce.7.cloned.1.call-done = f32[128,16,64]{0,2,1:T(8,128)} async-done(((f32[128,16,64]{0,2,1:T(8,128)}), f32[128,16,64]{0,2,1:T(8,128)}) %all-reduce.7.cloned.1.call-update) | async-done | bytes 524304 | tf_op jit(solution)/shard_map/psum | solution.py:136
  282.9 2.2 copy.213
  291.0 32.3 %all-reduce.9.cloned.1.call-done = bf16[3,128,1024]{1,2,0:T(8,128)(2,1)} async-done(((bf16[3,128,1024]{1,2,0:T(8,128)(2,1)}), bf16[3,128,1024]{1,2,0:T(8,128)(2,1)}) %all-reduce.9.cloned.1.call-update) | async-done | bytes 786448 | tf_op jit(solution)/shard_map/psum | solution.py:217
  326.6 2.3 copy.211
  336.9 2.5 add_convert_fusion.2
  341.7 13.4 %pad_maximum_fusion = bf16[1024,3072]{0,1:T(8,128)(2,1)} fusion(bf16[1024,1024]{0,1:T(8,128)(2,1)S(1)} %convolution_convert_fusion, bf16[1024,1024]{0,1:T(8,128)(2,1)S(1)} %convolution_convert_fusion.1, bf16[1024,1024]{0,1:T(8,128)(2,1)S(1)} %convolution_convert_fusion.2), kind=kLoop, calls=%fused_computation | loop fusion | flops 18874368 | bytes 12582912 | tf_op jit(solution)/shard_map/concatenate | solution.py:248
  355.4 58.3 %reduce-scatter.3.cloned.1.call-done = bf16[256,3072]{0,1:T(8,128)(2,1)} async-done(((bf16[1024,3072]{0,1:T(8,128)(2,1)}), bf16[256,3072]{0,1:T(8,128)(2,1)}) %reduce-scatter.3.cloned.1.call-update) | async-done | bytes 1572880 | tf_op jit(solution)/shard_map/reduce_scatter | solution.py:247
  422.0 2.2 fusion.36
  428.4 22.9 %reduce-scatter.5.cloned.1.call-done = bf16[256,3,256]{0,2,1:T(8,128)(2,1)} async-done(((bf16[256,3,1024]{0,2,1:T(8,128)(2,1)}), bf16[256,3,256]{0,2,1:T(8,128)(2,1)}) %reduce-scatter.5.cloned.1.call-update) | async-done | bytes 393232 | tf_op jit(solution)/shard_map/reduce_scatter | solution.py:262
  (244 shorter events, 108.4 us)
Async XLA Ops:
  7.2 51.1 %copy-start = (bf16[1,128,1024]{2,1,0:T(8,128)(2,1)S(1)}, bf16[1,128,1024]{2,1,0:T(8,128)(2,1)}, u32[]{:S(2)}) copy-start(bf16[1,128,1024]{2,1,0:T(8,128)(2,1)} %param.10) | copy-start | bytes 786436
  7.2 15.0 %copy-start.47 = (s32[1,2]{1,0:T(1,128)S(1)}, s32[1,2]{1,0:T(1,128)}, u32[]{:S(2)}) copy-start(s32[1,2]{1,0:T(1,128)} %param.11) | copy-start | bytes 28
  7.2 51.1 %all-gather.4.cloned.1.call-start = ((), (), s32[]{:S(2)}) async-start(), calls=%async_computation.2 | async-start | bytes 2621440 | tf_op jit(solution)/shard_map/all_gather | solution.py:49
  7.9 96.9 %all-gather.8.cloned.1.call-start = ((), (), s32[]{:S(2)}) async-start(), calls=%async_computation.4 | async-start | bytes 2621440 | tf_op jit(solution)/shard_map/all_gather | solution.py:48
  8.7 142.4 %all-gather.6.cloned.1.call-start = ((), (), s32[]{:S(2)}) async-start(), calls=%async_computation.3 | async-start | bytes 2621440 | tf_op jit(solution)/shard_map/all_gather | solution.py:47
  9.4 183.2 %all-reduce.11.cloned.1.call-start = ((), (), s32[]{:S(2)}) async-start(), calls=%async_computation.9 | async-start | bytes 2097152 | tf_op jit(solution)/shard_map/psum | solution.py:70
  106.9 46.3 %copy-start.37 = (bf16[1,128,1024]{2,1,0:T(8,128)(2,1)S(1)}, bf16[1,128,1024]{2,1,0:T(8,128)(2,1)}, u32[]{:S(2)}) copy-start(bf16[1,128,1024]{2,1,0:T(8,128)(2,1)} %param.15) | copy-start | bytes 786436
  107.7 56.7 %collective-permute-start = (bf16[2,64,1024]{2,1,0:T(8,128)(2,1)}, bf16[2,64,1024]{2,1,0:T(8,128)(2,1)}, u32[]{:S(2)}, u32[]{:S(2)}) collective-permute-start(bf16[2,64,1024]{2,1,0:T(8,128)(2,1)} %get-tuple-element.68), channel_id=1, source_target_pairs={{0,4},{4,8},{8,12},{1,5},{5,9},{9,13},{2,6},{6,10},{10,14},{3,7},{... | collective-permute-start | bytes 786440 | tf_op jit(solution)/shard_map/ppermute | solution.py:17
  110.1 54.3 %collective-permute-start.1 = (bf16[2,64,1024]{2,1,0:T(8,128)(2,1)}, bf16[2,64,1024]{2,1,0:T(8,128)(2,1)}, u32[]{:S(2)}, u32[]{:S(2)}) collective-permute-start(bf16[2,64,1024]{2,1,0:T(8,128)(2,1)} %get-tuple-element.69), channel_id=1, source_target_pairs={{4,0},{8,4},{12,8},{5,1},{9,5},{13,9},{6,2},{10,6},{14,10},{7,3},{... | collective-permute-start | bytes 786440 | tf_op jit(solution)/shard_map/ppermute | solution.py:20
  157.6 120.2 %all-reduce.7.cloned.1.call-start = ((), (), s32[]{:S(2)}) async-start(), calls=%async_computation.5 | async-start | bytes 1048576 | tf_op jit(solution)/shard_map/psum | solution.py:136
  161.8 10.3 %copy-start.21 = (bf16[2,64,16,64]{1,3,2,0:T(8,128)(2,1)}, bf16[2,64,16,64]{1,3,2,0:T(8,128)(2,1)S(1)}, u32[]{:S(2)}) copy-start(bf16[2,64,16,64]{1,3,2,0:T(8,128)(2,1)S(1)} %copy.197) | copy-start | bytes 786436
  194.6 5.9 %copy-start.36 = (bf16[1,128,1024]{1,2,0:T(8,128)(2,1)}, bf16[1,128,1024]{1,2,0:T(8,128)(2,1)S(1)}, u32[]{:S(2)}) copy-start(bf16[1,128,1024]{1,2,0:T(8,128)(2,1)S(1)} %copy.178) | copy-start | bytes 786436
  228.5 13.7 %copy-start.34 = (bf16[128,1024]{0,1:T(8,128)(2,1)S(1)}, bf16[128,1024]{0,1:T(8,128)(2,1)}, u32[]{:S(2)}) copy-start(bf16[128,1024]{0,1:T(8,128)(2,1)} %copy.162) | copy-start | bytes 786436
  229.5 13.8 %copy-start.12 = (bf16[1,128,1024]{1,2,0:T(8,128)(2,1)}, bf16[1,128,1024]{1,2,0:T(8,128)(2,1)S(1)}, u32[]{:S(2)}) copy-start(bf16[1,128,1024]{1,2,0:T(8,128)(2,1)S(1)} %copy.163) | copy-start | bytes 786436
  229.9 13.4 %copy-start.46 = (bf16[128,16,64]{0,2,1:T(8,128)(2,1)S(1)}, bf16[128,16,64]{0,2,1:T(8,128)(2,1)}, u32[]{:S(2)}) copy-start(bf16[128,16,64]{0,2,1:T(8,128)(2,1)} %get-tuple-element.30) | copy-start | bytes 786436
  243.3 80.0 %all-reduce.9.cloned.1.call-start = ((), (), s32[]{:S(2)}) async-start(), calls=%async_computation.6 | async-start | bytes 1572864 | tf_op jit(solution)/shard_map/psum | solution.py:217
  247.5 41.3 %collective-permute-start.2 = (bf16[2,64,1024]{2,1,0:T(8,128)(2,1)}, bf16[2,64,1024]{2,1,0:T(8,128)(2,1)}, u32[]{:S(2)}, u32[]{:S(2)}) collective-permute-start(bf16[2,64,1024]{2,1,0:T(8,128)(2,1)} %fusion.55), channel_id=1, source_target_pairs={{0,4},{4,8},{8,12},{1,5},{5,9},{9,13},{2,6},{6,10},{10,14},{3,7},{... | collective-permute-start | bytes 786440 | tf_op jit(solution)/shard_map/ppermute | solution.py:17
  249.7 39.1 %collective-permute-start.3 = (bf16[2,64,1024]{2,1,0:T(8,128)(2,1)}, bf16[2,64,1024]{2,1,0:T(8,128)(2,1)}, u32[]{:S(2)}, u32[]{:S(2)}) collective-permute-start(bf16[2,64,1024]{2,1,0:T(8,128)(2,1)} %fusion.56), channel_id=1, source_target_pairs={{4,0},{8,4},{12,8},{5,1},{9,5},{13,9},{6,2},{10,6},{14,10},{7,3},{... | collective-permute-start | bytes 786440 | tf_op jit(solution)/shard_map/ppermute | solution.py:20
  253.8 25.2 %copy-start.35 = (bf16[128,1024]{0,1:T(8,128)(2,1)S(1)}, bf16[128,1024]{0,1:T(8,128)(2,1)}, u32[]{:S(2)}) copy-start(bf16[128,1024]{0,1:T(8,128)(2,1)} %copy.162) | copy-start | bytes 786436
  288.6 125.2 %reduce-scatter.3.cloned.1.call-start = ((), (), s32[]{:S(2)}) async-start(), calls=%async_computation.7 | async-start | bytes 7864320 | tf_op jit(solution)/shard_map/reduce_scatter | solution.py:247
  289.9 34.7 %copy-start.11 = (bf16[1,128,1024]{1,2,0:T(8,128)(2,1)S(1)}, bf16[1,128,1024]{1,2,0:T(8,128)(2,1)}, u32[]{:S(2)}) copy-start(bf16[1,128,1024]{1,2,0:T(8,128)(2,1)} %copy-done.10) | copy-start | bytes 786436
  355.1 58.9 %copy-start.20 = (f32[16,64,128]{2,1,0:T(8,128)S(1)}, f32[16,64,128]{2,1,0:T(8,128)}, u32[]{:S(2)}) copy-start(f32[16,64,128]{2,1,0:T(8,128)} %fusion.49) | copy-start | bytes 1572868
  355.2 59.9 %copy-start.39 = (bf16[2,64,16,64]{1,3,2,0:T(8,128)(2,1)S(1)}, bf16[2,64,16,64]{1,3,2,0:T(8,128)(2,1)}, u32[]{:S(2)}) copy-start(bf16[2,64,16,64]{1,3,2,0:T(8,128)(2,1)} %get-tuple-element.93) | copy-start | bytes 786436
  355.2 96.2 %reduce-scatter.5.cloned.1.call-start = ((), (), s32[]{:S(2)}) async-start(), calls=%async_computation.8 | async-start | bytes 1966080 | tf_op jit(solution)/shard_map/reduce_scatter | solution.py:262
  (36 other events, 86.6 us)
Sparse Core Ops, SparseCore 0:
  9.6 48.6 all-gather.3
  59.8 44.9 all-gather.7
  106.4 44.6 all-gather.5
  157.7 34.8 all-reduce.10
  243.4 34.3 all-reduce.6
  288.7 34.6 all-reduce.8
  355.3 58.3 reduce-scatter.2
  416.0 35.2 reduce-scatter.4
where the time goes:
time: 465 us; the launch traced here: 460 us
  waiting for transfers between devices  274 us (59%)
  local copies, waits for them, and re-layouts  69.4 us (15%)
  other arithmetic  42.1 us (9%)
  matrix products  35.6 us (8%)
  between operations  19.4 us (4%)
  blocking collectives  12.1 us (3%)
  starting transfers between devices  8.24 us (2%)
    reduce_scatter x1, waiting for transfers between devices, per_device(): lax.psum_scatter(jnp.concatenate([lax.dot_general(grad, inputs, (((0,), (...  58.3 us
    all_gather x1, waiting for transfers between devices, per_device(): lax.all_gather(w_key, 'dp', axis=0, tiled=True)  44.5 us
    all_gather x1, waiting for transfers between devices, per_device(): lax.all_gather(w_query, 'dp', axis=0, tiled=True)  39.7 us
    all_gather x1, waiting for transfers between devices, per_device(): lax.all_gather(w_value, 'dp', axis=0, tiled=True)  35.5 us
    psum x1, waiting for transfers between devices, per_device(): lax.psum(jnp.stack([part_query_grad.reshape(2 * BLK, model_width), far_gr...  32.3 us
    reduce_scatter x1, waiting for transfers between devices, per_device(): lax.psum_scatter(reduced.astype(jnp.bfloat16), 'dp', scatter_dimension=2,...  22.9 us
    psum x1, waiting for transfers between devices, per_device(): global_sum, global_acc = lax.psum((part_sum, part_out), 'ctx')  21.1 us
    psum x1, waiting for transfers between devices, per_device(): lax.psum(picked.astype(jnp.bfloat16), 'ctx').astype(jnp.float32)  17.1 us
  transfers between devices with their start and end apart: 12, of which 8 were waited for; matrix products, arithmetic and copies ran while one was open for 16% of the time, Pallas kernels for 0%

commit v1 on v0

--- a/solution.py
+++ b/solution.py
@@ -7,6 +7,27 @@
 HEADS = 16
 BLK = 64
 NEG = -1e30
+
+
+def joined_along(blocks, dim):
+    blocks = jnp.moveaxis(blocks, 0, dim)
+    dims = blocks.shape
+    return blocks.reshape(*dims[:dim], dims[dim] * dims[dim + 1], *dims[dim + 2 :])
+
+
+def grow_blocks(shard, axis):
+    size, index = (lax.axis_size(axis), lax.axis_index(axis))
+    blocks, bit = (shard[None], 1)
+    while bit < size:
+        other = lax.ppermute(blocks, axis, [(i, i ^ bit) for i in range(size)])
+        low = index & bit == 0
+        blocks = jnp.concatenate([jnp.where(low, blocks, other), jnp.where(low, other, blocks)])
+        bit *= 2
+    return blocks
+
+
+def gather_by_bits(x, axis, dim):
+    return joined_along(grow_blocks(x, axis), dim)
 
 
 def with_halo(block, sides, width):
@@ -45,7 +66,7 @@
     chosen_blocks = global_blocks[0]
     pieces = (
         lax.all_gather(w_query, "dp", axis=0, tiled=True),
-        lax.all_gather(w_key, "dp", axis=0, tiled=True),
+        gather_by_bits(w_key, "dp", 0),
         lax.all_gather(w_value, "dp", axis=0, tiled=True),
     )
     projected = tuple(

time: 465 us -> 500 us (1.075)
  waiting for transfers between devices: 274 us -> 299 us
  starting transfers between devices: 8.24 us -> 17.8 us
    ppermute x0 -> x2, waiting for transfers between devices: none -> 71.4 us  [grow_blocks(): other = lax.ppermute(blocks, axis, [(i, i ^ bit) for i in range(size)])]
    all_gather x1, waiting for transfers between devices: 35.5 us -> 0.02 us  [per_device(): lax.all_gather(w_value, 'dp', axis=0, tiled=True)]
    ppermute x0 -> x2, starting transfers between devices: none -> 9.98 us  [grow_blocks(): other = lax.ppermute(blocks, axis, [(i, i ^ bit) for i in range(size)])]
    all_gather x1, waiting for transfers between devices: 39.7 us -> 29.9 us  [per_device(): lax.all_gather(w_query, 'dp', axis=0, tiled=True)]
    reduce_scatter x1, waiting for transfers between devices: 22.9 us -> 32.3 us  [per_device(): lax.psum_scatter(reduced.astype(jnp.bfloat16), 'dp', scatter_dimension=2,...]
    all_gather x1, waiting for transfers between devices: 44.5 us -> 35.3 us  [per_device(): pieces = lax.all_gather((w_query, w_key, w_value), 'dp', axis=0, tiled=True)]
  transfers between devices with their start and end apart: 12 -> 14, of which waited for: 8 -> 9; matrix products, arithmetic and copies ran while one was open for 16% -> 15% of each run, Pallas kernels for 0% -> 0%
where the time goes in v1:
time: 500 us; the launch traced here: 495 us
  waiting for transfers between devices  299 us (60%)
  local copies, waits for them, and re-layouts  66.9 us (13%)
  other arithmetic  44.1 us (9%)
  matrix products  35.6 us (7%)
  between operations  19.4 us (4%)
  starting transfers between devices  17.8 us (4%)
  blocking collectives  12.1 us (2%)
    ppermute x2, waiting for transfers between devices, grow_blocks(): other = lax.ppermute(blocks, axis, [(i, i ^ bit) for i in range(size)])  71.4 us
    reduce_scatter x1, waiting for transfers between devices, per_device(): lax.psum_scatter(jnp.concatenate([lax.dot_general(grad, inputs, (((0,), (...  57.5 us
    all_gather x1, waiting for transfers between devices, per_device(): pieces = lax.all_gather((w_query, w_key, w_value), 'dp', axis=0, tiled=True)  35.3 us
    reduce_scatter x1, waiting for transfers between devices, per_device(): lax.psum_scatter(reduced.astype(jnp.bfloat16), 'dp', scatter_dimension=2,...  32.3 us
    psum x1, waiting for transfers between devices, per_device(): lax.psum(jnp.stack([part_query_grad.reshape(2 * BLK, model_width), far_gr...  32.3 us
    all_gather x1, waiting for transfers between devices, per_device(): lax.all_gather(w_query, 'dp', axis=0, tiled=True)  29.9 us
    psum x1, waiting for transfers between devices, per_device(): global_sum, global_acc = lax.psum((part_sum, part_out), 'ctx')  21.1 us
    psum x1, waiting for transfers between devices, per_device(): lax.psum(picked.astype(jnp.bfloat16), 'ctx').astype(jnp.float32)  17.9 us
  transfers between devices with their start and end apart: 14, of which 9 were waited for; matrix products, arithmetic and copies ran while one was open for 15% of the time, Pallas kernels for 0%

profile of v1, /device:TPU:0, one launch (start us, length us, event | category | flops | bytes accessed | tf_op | source)
XLA Modules:
  0.0 495.1 jit_solution(12069661539932396160)
XLA Ops:
  8.0 3.1 collective-permute-start
  11.8 13.7 %collective-permute-done = bf16[1,256,1024]{2,1,0:T(8,128)(2,1)S(1)} collective-permute-done((bf16[1,256,1024]{2,1,0:T(8,128)(2,1)}, bf16[1,256,1024]{2,1,0:T(8,128)(2,1)S(1)}, u32[]{:S(2)}, u32[]{:S(2)}) %collective-permute-start) | collective-permute-done | bytes 524320 | tf_op jit(solution)/shard_map/ppermute | solution.py:22
  27.7 6.9 %collective-permute-start.1 = (bf16[2,256,1024]{2,1,0:T(8,128)(2,1)}, bf16[2,256,1024]{2,1,0:T(8,128)(2,1)S(1)}, u32[]{:S(2)}, u32[]{:S(2)}) collective-permute-start(bf16[2,256,1024]{2,1,0:T(8,128)(2,1)} %pad_maximum_fusion.2), channel_id=1, source_target_pairs={{0,2},{1,3},{2,0},{3,1},{4,6},{5,7},{6,4},{7,5},{8,10},{9,11},{10,... | collective-permute-start | bytes 3145736 | tf_op jit(solution)/shard_map/ppermute | solution.py:22
  41.8 2.5 compare_and_fusion.1
  44.9 57.7 %collective-permute-done.1 = bf16[2,256,1024]{2,1,0:T(8,128)(2,1)S(1)} collective-permute-done((bf16[2,256,1024]{2,1,0:T(8,128)(2,1)}, bf16[2,256,1024]{2,1,0:T(8,128)(2,1)S(1)}, u32[]{:S(2)}, u32[]{:S(2)}) %collective-permute-start.1) | collective-permute-done | bytes 1048608 | tf_op jit(solution)/shard_map/ppermute | solution.py:22
  109.5 29.9 %all-gather.6.cloned.1.call-done = bf16[1024,1024]{1,0:T(8,128)(2,1)} async-done(((bf16[256,1024]{1,0:T(8,128)(2,1)}), bf16[1024,1024]{1,0:T(8,128)(2,1)}) %all-gather.6.cloned.1.call-update) | async-done | bytes 2097168 | tf_op jit(solution)/shard_map/all_gather | solution.py:68
  159.6 3.5 fusion
  163.1 17.9 %all-reduce.11.cloned.1.call-done = (bf16[3,128,1024]{2,1,0:T(8,128)(2,1)}, bf16[128,16,64]{0,2,1:T(8,128)(2,1)}) async-done(((bf16[3,128,1024]{2,1,0:T(8,128)(2,1)}, bf16[128,16,64]{0,2,1:T(8,128)(2,1)}), (bf16[3,128,1024]{2,1,0:T(8,128)(2,1)}, bf16[128,16,64]{0,2,1:T(8,128)(2,1)})) %all-reduce.11.cloned.1.call-update) | async-done | bytes 1048592 | tf_op jit(solution)/shard_map/psum | solution.py:91
  183.9 2.5 fusion.14
  198.4 2.8 copy.198
  201.2 2.9 stack.46
  204.1 3.9 copy.199
  208.0 3.7 stack.47
  218.4 6.1 %pmax.7 = f32[16,128]{1,0:T(8,128)S(1)} all-reduce(f32[16,128]{1,0:T(8,128)S(1)} %get-tuple-element.95), channel_id=1, replica_groups=mesh['groups'=2,'ctx'=4,'dp'=4] {'ctx'}, use_global_device_ids=true, to_apply=%region_2.3 | all-reduce | flops 2048 | bytes 16384 | tf_op jit(solution)/shard_map/pmax | solution.py:148
  224.7 5.9 %psum.37 = f32[16,128]{1,0:T(8,128)S(1)} all-reduce(f32[16,128]{1,0:T(8,128)S(1)} %fusion.26), channel_id=1, replica_groups=mesh['groups'=2,'ctx'=4,'dp'=4] {'ctx'}, use_global_device_ids=true, to_apply=%region_5.6 | all-reduce | flops 2048 | bytes 16384 | tf_op jit(solution)/shard_map/psum | solution.py:157
  245.2 21.1 %all-reduce.7.cloned.1.call-done = f32[128,16,64]{0,2,1:T(8,128)} async-done(((f32[128,16,64]{0,2,1:T(8,128)}), f32[128,16,64]{0,2,1:T(8,128)}) %all-reduce.7.cloned.1.call-update) | async-done | bytes 524304 | tf_op jit(solution)/shard_map/psum | solution.py:157
  279.4 32.3 %all-reduce.9.cloned.1.call-done = bf16[3,128,1024]{1,2,0:T(8,128)(2,1)} async-done(((bf16[3,128,1024]{1,2,0:T(8,128)(2,1)}), bf16[3,128,1024]{1,2,0:T(8,128)(2,1)}) %all-reduce.9.cloned.1.call-update) | async-done | bytes 786448 | tf_op jit(solution)/shard_map/psum | solution.py:238
  325.3 2.5 add_convert_fusion.2
  330.1 13.4 %pad_maximum_fusion = bf16[1024,3072]{0,1:T(8,128)(2,1)} fusion(bf16[1024,1024]{0,1:T(8,128)(2,1)S(1)} %convolution_convert_fusion, bf16[1024,1024]{0,1:T(8,128)(2,1)S(1)} %convolution_convert_fusion.1, bf16[1024,1024]{0,1:T(8,128)(2,1)S(1)} %convolution_convert_fusion.2), kind=kLoop, calls=%fused_computation | loop fusion | flops 18874368 | bytes 12582912 | tf_op jit(solution)/shard_map/concatenate | solution.py:269
  344.6 57.5 %reduce-scatter.3.cloned.1.call-done = bf16[256,3072]{0,1:T(8,128)(2,1)} async-done(((bf16[1024,3072]{0,1:T(8,128)(2,1)}), bf16[256,3072]{0,1:T(8,128)(2,1)}) %reduce-scatter.3.cloned.1.call-update) | async-done | bytes 1572880 | tf_op jit(solution)/shard_map/reduce_scatter | solution.py:268
  410.4 3.1 fusion.36
  414.4 35.3 %all-gather.8.cloned.1.call-done = bf16[1024,1024]{1,0:T(8,128)(2,1)} async-done(((bf16[256,1024]{1,0:T(8,128)(2,1)}), bf16[1024,1024]{1,0:T(8,128)(2,1)}) %all-gather.8.cloned.1.call-update) | async-done | bytes 2097168 | tf_op jit(solution)/shard_map/all_gather | solution.py:261
  449.7 2.4 convolution_add_fusion.1
  453.7 32.3 %reduce-scatter.5.cloned.1.call-done = bf16[256,3,256]{0,2,1:T(8,128)(2,1)} async-done(((bf16[256,3,1024]{0,2,1:T(8,128)(2,1)}), bf16[256,3,256]{0,2,1:T(8,128)(2,1)}) %reduce-scatter.5.cloned.1.call-update) | async-done | bytes 393232 | tf_op jit(solution)/shard_map/reduce_scatter | solution.py:283
  (260 shorter events, 112.7 us)
Async XLA Ops:
  7.2 95.8 %copy-start = (bf16[1,128,1024]{2,1,0:T(8,128)(2,1)S(1)}, bf16[1,128,1024]{2,1,0:T(8,128)(2,1)}, u32[]{:S(2)}) copy-start(bf16[1,128,1024]{2,1,0:T(8,128)(2,1)} %param.10) | copy-start | bytes 786436
  7.2 96.3 %all-gather.4.cloned.1.call-start = ((), (), s32[]{:S(2)}) async-start(), calls=%async_computation.2 | async-start | bytes 2621440 | tf_op jit(solution)/shard_map/all_gather | solution.py:70
  7.9 131.5 %all-gather.6.cloned.1.call-start = ((), (), s32[]{:S(2)}) async-start(), calls=%async_computation.3 | async-start | bytes 2621440 | tf_op jit(solution)/shard_map/all_gather | solution.py:68
  8.0 17.5 %collective-permute-start = (bf16[1,256,1024]{2,1,0:T(8,128)(2,1)}, bf16[1,256,1024]{2,1,0:T(8,128)(2,1)S(1)}, u32[]{:S(2)}, u32[]{:S(2)}) collective-permute-start(bf16[1,256,1024]{2,1,0:T(8,128)(2,1)} %bitcast.338), channel_id=1, source_target_pairs={{0,1},{1,0},{2,3},{3,2},{4,5},{5,4},{6,7},{7,6},{8,9},{9,8},{10,11... | collective-permute-start | bytes 1572872 | tf_op jit(solution)/shard_map/ppermute | solution.py:22
  11.1 169.9 %all-reduce.11.cloned.1.call-start = ((), (), s32[]{:S(2)}) async-start(), calls=%async_computation.9 | async-start | bytes 2097152 | tf_op jit(solution)/shard_map/psum | solution.py:91
  11.8 26.5 %copy-start.36 = (bf16[1,128,1024]{2,1,0:T(8,128)(2,1)S(1)}, bf16[1,128,1024]{2,1,0:T(8,128)(2,1)}, u32[]{:S(2)}) copy-start(bf16[1,128,1024]{2,1,0:T(8,128)(2,1)} %param.15) | copy-start | bytes 786436
  27.7 74.9 %collective-permute-start.1 = (bf16[2,256,1024]{2,1,0:T(8,128)(2,1)}, bf16[2,256,1024]{2,1,0:T(8,128)(2,1)S(1)}, u32[]{:S(2)}, u32[]{:S(2)}) collective-permute-start(bf16[2,256,1024]{2,1,0:T(8,128)(2,1)} %pad_maximum_fusion.2), channel_id=1, source_target_pairs={{0,2},{1,3},{2,0},{3,1},{4,6},{5,7},{6,4},{7,5},{8,10},{9,11},{10,... | collective-permute-start | bytes 3145736 | tf_op jit(solution)/shard_map/ppermute | solution.py:22
  106.2 47.2 %collective-permute-start.2 = (bf16[2,64,1024]{2,1,0:T(8,128)(2,1)}, bf16[2,64,1024]{2,1,0:T(8,128)(2,1)}, u32[]{:S(2)}, u32[]{:S(2)}) collective-permute-start(bf16[2,64,1024]{2,1,0:T(8,128)(2,1)} %get-tuple-element.72), channel_id=1, source_target_pairs={{0,4},{4,8},{8,12},{1,5},{5,9},{9,13},{2,6},{6,10},{10,14},{3,7},{... | collective-permute-start | bytes 786440 | tf_op jit(solution)/shard_map/ppermute | solution.py:38
  108.2 45.2 %collective-permute-start.3 = (bf16[2,64,1024]{2,1,0:T(8,128)(2,1)S(1)}, bf16[2,64,1024]{2,1,0:T(8,128)(2,1)}, u32[]{:S(2)}, u32[]{:S(2)}) collective-permute-start(bf16[2,64,1024]{2,1,0:T(8,128)(2,1)S(1)} %get-tuple-element.73), channel_id=1, source_target_pairs={{4,0},{8,4},{12,8},{5,1},{9,5},{13,9},{6,2},{10,6},{14,10},{7,3},{... | collective-permute-start | bytes 786440 | tf_op jit(solution)/shard_map/ppermute | solution.py:41
  145.9 120.4 %all-reduce.7.cloned.1.call-start = ((), (), s32[]{:S(2)}) async-start(), calls=%async_computation.4 | async-start | bytes 1048576 | tf_op jit(solution)/shard_map/psum | solution.py:157
  159.6 27.6 %copy-start.48 = (bf16[2,64,16,64]{1,3,2,0:T(8,128)(2,1)}, bf16[2,64,16,64]{1,3,2,0:T(8,128)(2,1)S(1)}, u32[]{:S(2)}) copy-start(bf16[2,64,16,64]{1,3,2,0:T(8,128)(2,1)S(1)} %copy.170) | copy-start | bytes 786436
  231.8 80.0 %all-reduce.9.cloned.1.call-start = ((), (), s32[]{:S(2)}) async-start(), calls=%async_computation.5 | async-start | bytes 1572864 | tf_op jit(solution)/shard_map/psum | solution.py:238
  235.9 41.3 %collective-permute-start.4 = (bf16[2,64,1024]{2,1,0:T(8,128)(2,1)}, bf16[2,64,1024]{2,1,0:T(8,128)(2,1)}, u32[]{:S(2)}, u32[]{:S(2)}) collective-permute-start(bf16[2,64,1024]{2,1,0:T(8,128)(2,1)} %fusion.55), channel_id=1, source_target_pairs={{0,4},{4,8},{8,12},{1,5},{5,9},{9,13},{2,6},{6,10},{10,14},{3,7},{... | collective-permute-start | bytes 786440 | tf_op jit(solution)/shard_map/ppermute | solution.py:38
  238.2 39.0 %collective-permute-start.5 = (bf16[2,64,1024]{2,1,0:T(8,128)(2,1)}, bf16[2,64,1024]{2,1,0:T(8,128)(2,1)}, u32[]{:S(2)}, u32[]{:S(2)}) collective-permute-start(bf16[2,64,1024]{2,1,0:T(8,128)(2,1)} %fusion.56), channel_id=1, source_target_pairs={{4,0},{8,4},{12,8},{5,1},{9,5},{13,9},{6,2},{10,6},{14,10},{7,3},{... | collective-permute-start | bytes 786440 | tf_op jit(solution)/shard_map/ppermute | solution.py:41
  242.3 25.2 %copy-start.34 = (bf16[128,1024]{0,1:T(8,128)(2,1)S(1)}, bf16[128,1024]{0,1:T(8,128)(2,1)}, u32[]{:S(2)}) copy-start(bf16[128,1024]{0,1:T(8,128)(2,1)} %copy.162) | copy-start | bytes 786436
  277.0 125.2 %reduce-scatter.3.cloned.1.call-start = ((), (), s32[]{:S(2)}) async-start(), calls=%async_computation.7 | async-start | bytes 7864320 | tf_op jit(solution)/shard_map/reduce_scatter | solution.py:268
  278.3 34.7 %copy-start.10 = (bf16[1,128,1024]{1,2,0:T(8,128)(2,1)S(1)}, bf16[1,128,1024]{1,2,0:T(8,128)(2,1)}, u32[]{:S(2)}) copy-start(bf16[1,128,1024]{1,2,0:T(8,128)(2,1)} %copy-done.9) | copy-start | bytes 786436
  343.6 58.9 %copy-start.19 = (f32[16,64,128]{2,1,0:T(8,128)S(1)}, f32[16,64,128]{2,1,0:T(8,128)}, u32[]{:S(2)}) copy-start(f32[16,64,128]{2,1,0:T(8,128)} %fusion.49) | copy-start | bytes 1572868
  343.6 59.9 %copy-start.40 = (bf16[2,64,16,64]{1,3,2,0:T(8,128)(2,1)S(1)}, bf16[2,64,16,64]{1,3,2,0:T(8,128)(2,1)}, u32[]{:S(2)}) copy-start(bf16[2,64,16,64]{1,3,2,0:T(8,128)(2,1)} %get-tuple-element.97) | copy-start | bytes 786436
  343.6 106.1 %all-gather.8.cloned.1.call-start = ((), (), s32[]{:S(2)}) async-start(), calls=%async_computation.6 | async-start | bytes 2621440 | tf_op jit(solution)/shard_map/all_gather | solution.py:261
  344.3 141.7 %reduce-scatter.5.cloned.1.call-start = ((), (), s32[]{:S(2)}) async-start(), calls=%async_computation.8 | async-start | bytes 1966080 | tf_op jit(solution)/shard_map/reduce_scatter | solution.py:283
  413.5 36.1 %copy-start.39 = (bf16[128,1024]{1,0:T(8,128)(2,1)S(1)}, bf16[128,1024]{1,0:T(8,128)(2,1)}, u32[]{:S(2)}) copy-start(bf16[128,1024]{1,0:T(8,128)(2,1)} %get-tuple-element.85) | copy-start | bytes 786436
  414.4 37.7 %copy-start.1 = (bf16[1024,1024]{1,0:T(8,128)(2,1)S(1)}, bf16[1024,1024]{1,0:T(8,128)(2,1)}, u32[]{:S(2)}) copy-start(bf16[1024,1024]{1,0:T(8,128)(2,1)} %all-gather.4.cloned.1.call-done) | copy-start | bytes 6291460
  414.4 37.7 %copy-start.38 = (bf16[128,1024]{1,0:T(8,128)(2,1)S(1)}, bf16[128,1024]{1,0:T(8,128)(2,1)}, u32[]{:S(2)}) copy-start(bf16[128,1024]{1,0:T(8,128)(2,1)} %get-tuple-element.84) | copy-start | bytes 786436
  (42 other events, 170.0 us)
Sparse Core Ops, SparseCore 0:
  9.6 84.1 all-gather.3
  95.3 44.0 all-gather.5
  146.0 34.9 all-reduce.10
  231.9 34.3 all-reduce.6
  277.1 34.6 all-reduce.8
  343.7 58.3 reduce-scatter.2
  403.7 45.9 all-gather.7
  452.0 33.9 reduce-scatter.4
